TPU v7x, 32 devices: a whole 2x2x4 slice. The times are simulated.
32 devices in a mesh: rep: 2 (over y), ep: 8 (over z, x), tp: 2 (over core).
Axes of the slice: x: 2, y: 2, z: 4, core: 2. Of those that a mesh axis runs over, the one named last changes fastest.
Arguments:
- resid: bfloat16 [1024, 1440], P(('rep', 'ep')), parts along dimension 0, may hold values from -6 to 6
- query: bfloat16 [1024, 2048], P(('rep', 'ep'), 'tp'), parts along dimension 0, may hold values from -400 to 400
- key_value_pages: bfloat16 [2, 12288, 16, 256], P(None, ('rep', 'ep'), None, 'tp'), parts along dimension 1, may hold values from -4 to 4
- page_table: int32 [1024, 12], P(('rep', 'ep')), parts along dimension 0, may hold values from 0 to 767, as said below
- ctx_len: int32 [1024], P(('rep', 'ep')), parts along dimension 0, may hold values from 2 to 192, as said below
- experts_chosen: int32 [1024, 4], P(('rep', 'ep')), parts along dimension 0, may hold values from 0 to 7, as said below
- router_logits: float32 [1024, 4], P(('rep', 'ep')), parts along dimension 0, may hold values from -25 to 300
- norm_gain: float32 [1440], replicated, may hold values from 0.25 to 1.75
- out_proj: bfloat16 [2048, 1440], P('tp'), may hold values from -0.125 to 0.125
- w_gate: bfloat16 [8, 1440, 1440], P('ep', None, 'tp'), may hold values from -0.15625 to 0.15625
- w_up: bfloat16 [8, 1440, 1440], P('ep', None, 'tp'), may hold values from -0.15625 to 0.15625
- w_down: bfloat16 [8, 1440, 1440], P('ep', 'tp'), may hold values from -3 to 3
Outputs:
- mixed: bfloat16 [1024, 1440], P(('rep', 'ep'), 'tp'), parts along dimension 0
There are 2 independent parts, one for each index of `rep`. A program takes and returns all parts, laid end to end along the dimension named above; an argument that names none is the same for every part. Nothing has to cross between parts.
Inputs may be any that keep to these rules, and one draw needn't show every extreme that they name: Each block of 64 tokens holds its own pool: the rows of page_table of one block together name each of its 768 pages once. `ctx_len`: every block of 64 tokens has a token with 192 positions. `experts_chosen`: each row names 4 different experts. Within the rows of one device no expert is named by more than 64 rows, and one expert is named by exactly 64 of them.
All inputs are finite; a program needn't handle non-finite values.
Results may differ from a plain program's by a relative error of at most 0.008.
Values may be sent and summed in bfloat16 or wider, within the bound.
No kernel may reach another device: no remote copies, remote signals or barrier semaphores. Data moves between devices by JAX's collectives and lax.ppermute only.
A program may use at most 128 MiB of HBM per device.

v0:
```python
import math
import jax
import jax.numpy as jnp
from jax import lax
from jax.sharding import PartitionSpec as P

HEAD_WIDTH = 64


def body(
    resid,
    query,
    key_value_pages,
    page_table,
    ctx_len,
    experts_chosen,
    router_logits,
    norm_gain,
    out_proj,
    w_gate,
    w_up,
    w_down,
):
    tok_rows = query.shape[0]
    model_width = resid.shape[1]
    query_heads = query.shape[1] // HEAD_WIDTH
    cache_heads = key_value_pages.shape[3] // HEAD_WIDTH
    group_width = query_heads // cache_heads
    positions = page_table.shape[1] * key_value_pages.shape[2]
    cached_keys = key_value_pages[0][page_table].reshape(
        tok_rows, positions, cache_heads, HEAD_WIDTH
    )
    cached_values = key_value_pages[1][page_table].reshape(
        tok_rows, positions, cache_heads, HEAD_WIDTH
    )
    query_block = query.reshape(tok_rows, cache_heads, group_width, HEAD_WIDTH)
    scores = jnp.einsum(
        "tgqd,tpgd->tgqp", query_block, cached_keys, preferred_element_type=jnp.float32
    ) * (1.0 / math.sqrt(HEAD_WIDTH))
    visible = jnp.arange(positions, dtype=jnp.int32)[None, :] < ctx_len[:, None]
    scores = jnp.where(visible[:, None, None, :], scores, -jnp.inf)
    row_max = jnp.max(scores, axis=3, keepdims=True)
    weights = jnp.exp(scores - row_max)
    probability = (weights / jnp.sum(weights, axis=3, keepdims=True)).astype(jnp.bfloat16)
    attended = jnp.einsum(
        "tgqp,tpgd->tgqd", probability, cached_values, preferred_element_type=jnp.float32
    )
    attended = attended.astype(jnp.bfloat16).reshape(tok_rows, query_heads * HEAD_WIDTH)
    head_part = jnp.dot(attended, out_proj, preferred_element_type=jnp.float32)
    half_cols = model_width // lax.axis_size("tp")
    offset = lax.axis_index("tp") * half_cols
    share = lax.psum_scatter(head_part, "tp", scatter_dimension=1, tiled=True)
    stream = lax.dynamic_slice_in_dim(resid, offset, half_cols, 1).astype(jnp.float32) + share
    mean_square = lax.psum(jnp.sum(stream * stream, axis=1), "tp") / model_width
    gain_cols = lax.dynamic_slice_in_dim(norm_gain, offset, half_cols, 0)
    normed = (stream * lax.rsqrt(mean_square + 1e-05)[:, None] * gain_cols).astype(jnp.bfloat16)
    gate_weights = jax.nn.softmax(router_logits, axis=1)
    top_count = experts_chosen.shape[1]
    local_experts = w_gate.shape[0]
    owners = lax.axis_size("ep")
    experts = local_experts * owners
    capacity = max(2, min(tok_rows, 2 * tok_rows * top_count // experts))
    chosen_flat = experts_chosen.reshape(-1)
    onehot = (chosen_flat[:, None] == jnp.arange(experts, dtype=jnp.int32)[None, :]).astype(
        jnp.int32
    )
    before = jnp.cumsum(onehot, axis=0, dtype=jnp.int32) - onehot
    slot_rank = jnp.sum(before * onehot, axis=1, dtype=jnp.int32)
    slot_index = (chosen_flat * capacity + slot_rank).reshape(tok_rows, top_count)
    slot_range = jnp.arange(experts * capacity, dtype=jnp.int32)
    placed = slot_index[:, :, None] == slot_range[None, None, :]
    dispatch = jnp.sum(placed.astype(jnp.float32), axis=1).astype(jnp.bfloat16)
    outgoing = lax.dot_general(
        dispatch, normed, (((0,), (0,)), ((), ())), preferred_element_type=jnp.float32
    )
    outgoing = outgoing.astype(jnp.bfloat16).reshape(
        owners, local_experts, capacity, normed.shape[1]
    )
    arrived_full = lax.all_gather(
        lax.all_to_all(outgoing, "ep", split_axis=0, concat_axis=0, tiled=True),
        "tp",
        axis=3,
        tiled=True,
    )
    gate_value = jnp.einsum(
        "sekd,edf->sekf", arrived_full, w_gate, preferred_element_type=jnp.float32
    )
    up_value = jnp.einsum("sekd,edf->sekf", arrived_full, w_up, preferred_element_type=jnp.float32)
    hidden = (gate_value * jax.nn.sigmoid(1.702 * gate_value) * (up_value + 1.0)).astype(
        jnp.bfloat16
    )
    partial_value = jnp.einsum("sekf,efd->sekd", hidden, w_down, preferred_element_type=jnp.float32)
    finished = lax.psum_scatter(partial_value, "tp", scatter_dimension=3, tiled=True).astype(
        jnp.bfloat16
    )
    returned = lax.all_to_all(finished, "ep", split_axis=0, concat_axis=0, tiled=True)
    combine = jnp.sum(placed.astype(jnp.float32) * gate_weights[:, :, None], axis=1)
    expert_mix = jnp.dot(
        combine,
        returned.reshape(experts * capacity, -1).astype(jnp.float32),
        precision=lax.Precision.HIGHEST,
    )
    mixed = stream + expert_mix
    return mixed.astype(jnp.bfloat16)


def solution(mesh):
    return jax.shard_map(
        body,
        mesh=mesh,
        in_specs=(
            P(("rep", "ep"), None),
            P(("rep", "ep"), "tp"),
            P(None, ("rep", "ep"), None, "tp"),
            P(("rep", "ep"), None),
            P(("rep", "ep")),
            P(("rep", "ep"), None),
            P(("rep", "ep"), None),
            P(),
            P("tp", None),
            P("ep", None, "tp"),
            P("ep", None, "tp"),
            P("ep", "tp", None),
        ),
        out_specs=P(("rep", "ep"), "tp"),
        check_vma=False,
    )
```

profile of v0, /device:TPU:0, one launch (start us, length us, event | category | flops | bytes accessed | tf_op | source)
XLA Modules:
  0.0 195.1 jit_solution(847633869631142299)
XLA Ops:
  6.5 6.7 %slice_bitcast_fusion.1 = (bf16[768,16,128]{2,1,0:T(8,128)(2,1)}, bf16[768,16,128]{2,1,0:T(8,128)(2,1)}) fusion(bf16[2,768,16,128]{3,2,1,0:T(8,128)(2,1)} %param.14), kind=kLoop, calls=%fused_computation.9 | loop fusion | bytes 12582912 | tf_op jit(solution)/shard_map/squeeze | solution.py:30
  13.3 0.1 copy.53
  13.4 0.1 reshape.101
  13.5 4.9 %gather_fusion = bf16[768,16,128]{2,1,0:T(8,128)(2,1)} fusion(bf16[768,16,128]{2,1,0:T(8,128)(2,1)} %get-tuple-element.7, s32[1024]{0:T(1024)S(1)} %pad_clamp_fusion), kind=kCustom, calls=%fused_computation | custom fusion | bytes 6294528 | tf_op jit(solution)/shard_map/gather | solution.py:30
  18.3 11.7 %reshape.87 = bf16[64,192,2,64]{3,2,1,0:T(2,128)(2,1)} reshape(bf16[768,16,128]{2,1,0:T(8,128)(2,1)} %gather_fusion) | data formatting | bytes 6291456 | tf_op jit(solution)/shard_map/reshape | solution.py:30
  30.0 0.2 reshape.88
  30.2 0.1 iota_compare_fusion.1
  30.3 4.9 %gather_fusion.1 = bf16[768,16,128]{2,1,0:T(8,128)(2,1)} fusion(bf16[768,16,128]{2,1,0:T(8,128)(2,1)} %get-tuple-element.8, s32[1024]{0:T(1024)S(1)} %pad_clamp_fusion), kind=kCustom, calls=%fused_computation.1 | custom fusion | bytes 6294528 | tf_op jit(solution)/shard_map/gather | solution.py:33
  35.2 11.6 %reshape.89 = bf16[64,192,2,64]{3,2,1,0:T(2,128)(2,1)} reshape(bf16[768,16,128]{2,1,0:T(8,128)(2,1)} %gather_fusion.1) | data formatting | bytes 6291456 | tf_op jit(solution)/shard_map/reshape | solution.py:33
  46.8 7.3 %fusion.60 = (f32[64,2,8]{2,1,0:T(2,128)S(1)}, f32[64,2,8,192]{3,2,1,0:T(8,128)}) fusion(bf16[64,2,8,64]{3,2,1,0:T(8,128)(2,1)S(1)} %reshape.88, bf16[64,192,2,64]{3,2,1,0:T(2,128)(2,1)} %reshape.87, pred[64,192]{1,0:T(8,128)(4,1)S(1)} %iota_compare_fusion.1), kind=kOutput, calls=%fused_computation.69 | convolution fusion | flops 25952448 | bytes 4079616 | tf_op jit(solution)/shard_map/sub | solution.py:43
  54.1 4.9 %fusion.37 = bf16[64,2,8,64]{3,2,1,0:T(8,128)(2,1)S(1)} fusion(bf16[64,192,2,64]{3,2,1,0:T(2,128)(2,1)} %reshape.89, f32[64,2,8,192]{3,2,1,0:T(8,128)} %get-tuple-element.10, f32[64,2,8]{2,1,0:T(2,128)S(1)} %get-tuple-element.9), kind=kOutput, calls=%fused_computation.33 | convolution fusion | flops 25624576 | bytes 4067328 | tf_op jit(solution)/shard_map/tgqp,tpgd->tgqd/dot_general | solution.py:45
  59.0 0.2 reshape.90
  59.2 0.0 copy-start.7
  59.3 1.8 convolution_bitcast_fusion.1
  61.1 0.0 reduce-scatter.7.cloned.1.call-update
  61.1 0.2 all-gather.2.cloned.1.call-start
  61.3 0.1 copy.56
  61.4 0.1 eq.42
  61.5 0.1 eq.38
  61.7 0.6 reduce-window.6
  62.2 0.2 slice_reduce_fusion
  62.5 0.1 fusion.53
  62.6 0.1 reduce_sum.58
  62.7 0.1 copy.58
  62.8 0.1 dynamic_slice.7
  62.9 0.2 convert_reduce_fusion
  63.1 9.0 %reduce-scatter.7.cloned.1.call-done = f32[720,64]{1,0:T(8,128)} async-done(((f32[1440,64]{1,0:T(8,128)}), f32[720,64]{1,0:T(8,128)}) %reduce-scatter.7.cloned.1.call-update) | async-done | bytes 184336
  72.1 1.1 copy.65
  73.3 0.2 multiply_reduce_fusion
  73.5 2.5 %psum.7 = f32[64]{0:T(128)S(1)} all-reduce(f32[64]{0:T(128)S(1)} %multiply_reduce_fusion), channel_id=1, replica_groups=mesh['rep'=2,'ep'=8,'tp'=2] {'tp'}, use_global_device_ids=true, to_apply=%region_11.12 | all-reduce | flops 64 | bytes 512 | tf_op jit(solution)/shard_map/psum | solution.py:54
  75.9 0.5 convolution_convert_fusion
  76.4 0.3 copy.59
  76.7 26.2 %all_to_all.10 = bf16[8,1,64,720]{3,2,1,0:T(8,128)(2,1)S(1)} all-to-all(bf16[8,1,64,720]{3,2,1,0:T(8,128)(2,1)S(1)} %bitcast.116), channel_id=1, replica_groups=mesh['rep'=2,'ep'=8,'tp'=2] {'ep'}, dimensions={0} | all-to-all | bytes 1474560 | tf_op jit(solution)/shard_map/all_to_all | solution.py:80
  102.9 1.8 copy.61
  104.7 0.0 all-gather.2.cloned.1.call-update
  104.7 0.0 reduce-scatter.9.cloned.1.call-start
  104.8 11.0 %all-gather.2.cloned.1.call-done = bf16[8,1,64,1440]{2,0,1,3:T(8,128)(2,1)} async-done(((bf16[8,1,64,720]{2,0,1,3:T(8,128)(2,1)}), bf16[8,1,64,1440]{2,0,1,3:T(8,128)(2,1)}) %all-gather.2.cloned.1.call-update) | async-done | bytes 1474576 | tf_op jit(solution)/shard_map/all_gather | solution.py:79
  115.7 3.7 %copy.62 = bf16[8,1,64,1440]{3,2,0,1:T(8,128)(2,1)S(1)} copy(bf16[8,1,64,1440]{2,0,1,3:T(8,128)(2,1)} %all-gather.2.cloned.1.call-done) | data formatting | bytes 2949120 | tf_op jit(solution)/shard_map/all_gather | solution.py:79
  119.4 4.2 %fusion.8 = f32[8,64,720]{2,1,0:T(8,128)} fusion(bf16[1,1440,720]{2,1,0:T(8,128)(2,1)} %param.21, bf16[8,1,64,1440]{3,2,0,1:T(8,128)(2,1)S(1)} %copy.62), kind=kOutput, calls=%fused_computation.14 | convolution fusion | flops 1061683200 | bytes 5022720 | tf_op jit(solution)/shard_map/sekd,edf->sekf/dot_general | solution.py:85
  123.6 7.7 %convolution_bitcast_fusion = f32[8,1,64,1440]{3,2,0,1:T(8,128)} fusion(bf16[1,720,1440]{2,1,0:T(8,128)(2,1)} %param.23, bf16[1,1440,720]{2,1,0:T(8,128)(2,1)} %param.22, bf16[8,1,64,1440]{3,2,0,1:T(8,128)(2,1)S(1)} %copy.62, f32[8,64,720]{2,1,0:T(8,128)} %fusion.8), kind=kOutput, calls=%fused_computation.7 | convolution fusion | flops 2126315520 | bytes 10045440 | tf_op jit(solution)/shard_map/sekf,efd->sekd/dot_general | solution.py:92
  131.2 5.7 %copy.66 = f32[8,1,64,1440]{2,0,1,3:T(8,128)} copy(f32[8,1,64,1440]{3,2,0,1:T(8,128)} %convolution_bitcast_fusion) | data formatting | bytes 5898240
  137.0 5.9 %reshape.126 = f32[1440,512]{1,0:T(8,128)} reshape(f32[1440,1,8,64]{3,2,1,0:T(8,128)} %bitcast.113) | data formatting | bytes 5898240
  142.8 0.0 reduce-scatter.9.cloned.1.call-update
  142.9 12.2 %reduce-scatter.9.cloned.1.call-done = f32[720,512]{1,0:T(8,128)} async-done(((f32[1440,512]{1,0:T(8,128)}), f32[720,512]{1,0:T(8,128)}) %reduce-scatter.9.cloned.1.call-update) | async-done | bytes 1474576
  155.1 3.1 %reshape.127 = bf16[720,1,8,64]{3,2,1,0:T(8,128)(2,1)} reshape(f32[720,512]{1,0:T(8,128)} %reduce-scatter.9.cloned.1.call-done) | data formatting | bytes 2211840
  158.2 2.9 %copy.67 = bf16[8,1,64,720]{3,2,0,1:T(8,128)(2,1)} copy(bf16[8,1,64,720]{2,0,1,3:T(8,128)(2,1)} %bitcast.114) | data formatting | bytes 1474560
  161.1 26.3 %all_to_all.11 = bf16[8,1,64,720]{3,2,1,0:T(8,128)(2,1)S(1)} all-to-all(bf16[8,1,64,720]{3,2,1,0:T(8,128)(2,1)} %bitcast.117), channel_id=1, replica_groups=mesh['rep'=2,'ep'=8,'tp'=2] {'ep'}, dimensions={0} | all-to-all | bytes 1474560 | tf_op jit(solution)/shard_map/all_to_all | solution.py:96
  187.4 1.2 fusion.40
  (28 shorter events, 0.2 us)
Async XLA Ops:
  6.5 52.7 %copy-start = (bf16[1024,1440]{0,1:T(8,128)(2,1)S(1)}, bf16[1024,1440]{0,1:T(8,128)(2,1)}, u32[]{:S(2)}) copy-start(bf16[1024,1440]{0,1:T(8,128)(2,1)} %param.20) | copy-start | bytes 8847364
  6.5 6.7 %copy-start.6 = (s32[64,12]{0,1:T(8,128)S(1)}, s32[64,12]{0,1:T(8,128)}, u32[]{:S(2)}) copy-start(s32[64,12]{0,1:T(8,128)} %param.15) | copy-start | bytes 9220
  6.5 65.6 %reduce-scatter.7.cloned.1.call-start = ((), (), s32[]{:S(2)}) async-start(), calls=%async_computation.5 | async-start | bytes 1105920
  18.3 11.7 %copy-start.3 = (bf16[64,1024]{1,0:T(8,128)(2,1)S(1)}, bf16[64,1024]{1,0:T(8,128)(2,1)}, u32[]{:S(2)}) copy-start(bf16[64,1024]{1,0:T(8,128)(2,1)} %param.13) | copy-start | bytes 393220
  18.3 11.8 %copy-start.8 = (s32[64]{0:T(128)S(1)}, s32[64]{0:T(128)}, u32[]{:S(2)}) copy-start(s32[64]{0:T(128)} %param.16) | copy-start | bytes 772
  59.2 2.1 %copy-start.5 = (s32[64,4]{0,1:T(4,128)S(1)}, s32[64,4]{0,1:T(4,128)}, u32[]{:S(2)}) copy-start(s32[64,4]{0,1:T(4,128)} %param.17) | copy-start | bytes 3076
  59.2 3.5 %copy-start.7 = (f32[1440]{0:T(1024)S(1)}, f32[1440]{0:T(1024)}, u32[]{:S(2)}) copy-start(f32[1440]{0:T(1024)} %param.19) | copy-start | bytes 17284
  59.3 3.6 %copy-start.4 = (f32[64,4]{0,1:T(4,128)S(1)}, f32[64,4]{0,1:T(4,128)}, u32[]{:S(2)}) copy-start(f32[64,4]{0,1:T(4,128)} %param.18) | copy-start | bytes 3076
  59.3 14.0 %copy-start.2 = (bf16[64,1440]{1,0:T(8,128)(2,1)S(1)}, bf16[64,1440]{1,0:T(8,128)(2,1)}, u32[]{:S(2)}) copy-start(bf16[64,1440]{1,0:T(8,128)(2,1)} %param.12) | copy-start | bytes 552964
  61.1 54.6 %all-gather.2.cloned.1.call-start = ((), (), s32[]{:S(2)}) async-start(), calls=%async_computation.4 | async-start | bytes 4423680 | tf_op jit(solution)/shard_map/all_gather | solution.py:79
  104.7 50.4 %reduce-scatter.9.cloned.1.call-start = ((), (), s32[]{:S(2)}) async-start(), calls=%async_computation.6 | async-start | bytes 4423680
  158.2 30.4 %copy-start.1 = (bf16[1024,1440]{0,1:T(8,128)(2,1)S(1)}, bf16[1024,1440]{0,1:T(8,128)(2,1)}, u32[]{:S(2)}) copy-start(bf16[1024,1440]{0,1:T(8,128)(2,1)} %param.20) | copy-start | bytes 8847364
Sparse Core Ops, SparseCore 0:
  61.2 10.8 reduce-scatter.6
  104.9 10.8 all-gather.1
  143.0 12.0 reduce-scatter.8
where the time goes:
time: 196 us; the launch traced here: 195 us
  local copies, waits for them, and re-layouts  65.6 us (33%)
  blocking collectives  54.9 us (28%)
  waiting for transfers between devices  32.2 us (16%)
  matrix products  27.5 us (14%)
  between operations  13.3 us (7%)
    all_to_all x1, blocking collectives, body(): lax.all_to_all(finished, 'ep', split_axis=0, concat_axis=0, tiled=True)  26.3 us
    all_to_all x1, blocking collectives, body(): lax.all_to_all(outgoing, 'ep', split_axis=0, concat_axis=0, tiled=True)  26.2 us
    unnamed x5, waiting for transfers between devices  21.3 us
    unnamed x24, local copies, waits for them, and re-layouts  18.9 us
    reshape x1, local copies, waits for them, and re-layouts, body(): key_value_pages[0][page_table]  11.7 us
    reshape x1, local copies, waits for them, and re-layouts, body(): key_value_pages[1][page_table]  11.6 us
    all_gather x1, waiting for transfers between devices, body(): lax.all_gather(lax.all_to_all(outgoing, 'ep', split_axis=0, concat_axis=0...  11 us
    dot_general x1, matrix products, body(): jnp.einsum('sekf,efd->sekd', hidden, w_down, preferred_element_type=jnp.f...  7.66 us
  transfers between devices with their start and end apart: 3, of which 3 were waited for; matrix products, arithmetic and copies ran while one was open for 1% of the time, Pallas kernels for 0%

commit v1 on v0

--- a/solution.py
+++ b/solution.py
@@ -76,11 +76,17 @@
     outgoing = outgoing.astype(jnp.bfloat16).reshape(
         owners, local_experts, capacity, normed.shape[1]
     )
-    arrived_full = lax.all_gather(
-        lax.all_to_all(outgoing, "ep", split_axis=0, concat_axis=0, tiled=True),
-        "tp",
+    arrived_full = jnp.concatenate(
+        lax.all_to_all(
+            jnp.stack(
+                [lax.all_to_all(outgoing, "ep", split_axis=0, concat_axis=0, tiled=True)]
+                * lax.axis_size("tp")
+            ),
+            "tp",
+            0,
+            0,
+        ),
         axis=3,
-        tiled=True,
     )
     gate_value = jnp.einsum(
         "sekd,edf->sekf", arrived_full, w_gate, preferred_element_type=jnp.float32

time: 196 us -> 187 us (0.954)
  waiting for transfers between devices: 32.2 us -> 19.1 us
  blocking collectives: 54.9 us -> 59.9 us
    all_gather x1 -> x0, waiting for transfers between devices: 11 us -> none  [body(): lax.all_gather(lax.all_to_all(outgoing, 'ep', split_axis=0, concat_axis=0...]
    all_to_all x0 -> x1, blocking collectives: none -> 5 us  [body(): lax.all_to_all(jnp.stack([lax.all_to_all(outgoing, 'ep', split_axis=0, co...]
    all_gather x1 -> x0, local copies, waits for them, and re-layouts: 3.66 us -> none  [body(): lax.all_gather(lax.all_to_all(outgoing, 'ep', split_axis=0, concat_axis=0...]
    unnamed x5 -> x4, waiting for transfers between devices: 21.3 us -> 19.1 us
    another operation x1 -> x2, local copies, waits for them, and re-layouts: 0.01 us -> 2.11 us
    unnamed x24 -> x26, local copies, waits for them, and re-layouts: 18.9 us -> 18.9 us
  transfers between devices with their start and end apart: 3 -> 2, of which waited for: 3 -> 2; matrix products, arithmetic and copies ran while one was open for 1% -> 1% of each run, Pallas kernels for 0% -> 0%
where the time goes in v1:
time: 187 us; the launch traced here: 186 us
  local copies, waits for them, and re-layouts  63.9 us (34%)
  blocking collectives  59.9 us (32%)
  matrix products  28.1 us (15%)
  waiting for transfers between devices  19.1 us (10%)
  between operations  13.6 us (7%)
    all_to_all x1, blocking collectives, body(): lax.all_to_all(finished, 'ep', split_axis=0, concat_axis=0, tiled=True)  26.3 us
    all_to_all x1, blocking collectives, body(): lax.all_to_all(outgoing, 'ep', split_axis=0, concat_axis=0, tiled=True)  26.2 us
    unnamed x4, waiting for transfers between devices  19.1 us
    unnamed x26, local copies, waits for them, and re-layouts  18.9 us
    reshape x1, local copies, waits for them, and re-layouts, body(): key_value_pages[0][page_table]  11.7 us
    reshape x1, local copies, waits for them, and re-layouts, body(): key_value_pages[1][page_table]  11.6 us
    dot_general x1, matrix products, body(): jnp.einsum('sekf,efd->sekd', hidden, w_down, preferred_element_type=jnp.f...  7.66 us
    sub x1, matrix products, body(): weights = jnp.exp(scores - row_max)  7.32 us
  transfers between devices with their start and end apart: 2, of which 2 were waited for; matrix products, arithmetic and copies ran while one was open for 1% of the time, Pallas kernels for 0%

profile of v1, /device:TPU:0, one launch (start us, length us, event | category | flops | bytes accessed | tf_op | source)
XLA Modules:
  0.0 186.2 jit_solution(17113803546833560919)
XLA Ops:
  6.5 6.7 %slice_bitcast_fusion.1 = (bf16[768,16,128]{2,1,0:T(8,128)(2,1)}, bf16[768,16,128]{2,1,0:T(8,128)(2,1)}) fusion(bf16[2,768,16,128]{3,2,1,0:T(8,128)(2,1)} %param.14), kind=kLoop, calls=%fused_computation.9 | loop fusion | bytes 12582912 | tf_op jit(solution)/shard_map/squeeze | solution.py:30
  13.3 0.1 copy.52
  13.4 0.1 reshape.108
  13.5 4.9 %gather_fusion = bf16[768,16,128]{2,1,0:T(8,128)(2,1)} fusion(bf16[768,16,128]{2,1,0:T(8,128)(2,1)} %get-tuple-element.7, s32[1024]{0:T(1024)S(1)} %pad_clamp_fusion), kind=kCustom, calls=%fused_computation | custom fusion | bytes 6294528 | tf_op jit(solution)/shard_map/gather | solution.py:30
  18.3 11.7 %reshape.93 = bf16[64,192,2,64]{3,2,1,0:T(2,128)(2,1)} reshape(bf16[768,16,128]{2,1,0:T(8,128)(2,1)} %gather_fusion) | data formatting | bytes 6291456 | tf_op jit(solution)/shard_map/reshape | solution.py:30
  30.0 0.2 reshape.94
  30.2 0.1 iota_compare_fusion.1
  30.3 4.9 %gather_fusion.1 = bf16[768,16,128]{2,1,0:T(8,128)(2,1)} fusion(bf16[768,16,128]{2,1,0:T(8,128)(2,1)} %get-tuple-element.8, s32[1024]{0:T(1024)S(1)} %pad_clamp_fusion), kind=kCustom, calls=%fused_computation.1 | custom fusion | bytes 6294528 | tf_op jit(solution)/shard_map/gather | solution.py:33
  35.2 11.6 %reshape.95 = bf16[64,192,2,64]{3,2,1,0:T(2,128)(2,1)} reshape(bf16[768,16,128]{2,1,0:T(8,128)(2,1)} %gather_fusion.1) | data formatting | bytes 6291456 | tf_op jit(solution)/shard_map/reshape | solution.py:33
  46.8 7.3 %fusion.52 = (f32[64,2,8]{2,1,0:T(2,128)S(1)}, f32[64,2,8,192]{3,2,1,0:T(8,128)}) fusion(bf16[64,2,8,64]{3,2,1,0:T(8,128)(2,1)S(1)} %reshape.94, bf16[64,192,2,64]{3,2,1,0:T(2,128)(2,1)} %reshape.93, pred[64,192]{1,0:T(8,128)(4,1)S(1)} %iota_compare_fusion.1), kind=kOutput, calls=%fused_computation.68 | convolution fusion | flops 25952448 | bytes 4079616 | tf_op jit(solution)/shard_map/sub | solution.py:43
  54.1 4.9 %fusion.31 = bf16[64,2,8,64]{3,2,1,0:T(8,128)(2,1)S(1)} fusion(bf16[64,192,2,64]{3,2,1,0:T(2,128)(2,1)} %reshape.95, f32[64,2,8,192]{3,2,1,0:T(8,128)} %get-tuple-element.10, f32[64,2,8]{2,1,0:T(2,128)S(1)} %get-tuple-element.9), kind=kOutput, calls=%fused_computation.32 | convolution fusion | flops 25624576 | bytes 4067328 | tf_op jit(solution)/shard_map/tgqp,tpgd->tgqd/dot_general | solution.py:45
  59.0 0.2 reshape.96
  59.2 0.0 copy-start.8
  59.3 0.0 copy-start.5
  59.3 1.8 convolution_bitcast_fusion.1
  61.1 0.0 reduce-scatter.7.cloned.1.call-update
  61.1 0.2 reduce-scatter.9.cloned.1.call-start
  61.3 0.1 copy.55
  61.4 0.1 eq.42
  61.5 0.1 eq.38
  61.7 0.6 reduce-window.6
  62.2 0.2 slice_reduce_fusion
  62.5 0.1 fusion.45
  62.6 0.1 reduce_sum.58
  62.7 0.1 copy.57
  62.8 0.1 dynamic_slice.7
  62.9 0.2 convert_reduce_fusion
  63.1 9.0 %reduce-scatter.7.cloned.1.call-done = f32[720,64]{1,0:T(8,128)} async-done(((f32[1440,64]{1,0:T(8,128)}), f32[720,64]{1,0:T(8,128)}) %reduce-scatter.7.cloned.1.call-update) | async-done | bytes 184336
  72.1 1.1 copy.63
  73.3 0.2 multiply_reduce_fusion
  73.5 2.5 %psum.7 = f32[64]{0:T(128)S(1)} all-reduce(f32[64]{0:T(128)S(1)} %multiply_reduce_fusion), channel_id=1, replica_groups=mesh['rep'=2,'ep'=8,'tp'=2] {'tp'}, use_global_device_ids=true, to_apply=%region_11.12 | all-reduce | flops 64 | bytes 512 | tf_op jit(solution)/shard_map/psum | solution.py:54
  75.9 0.5 convolution_convert_fusion
  76.4 0.3 copy.58
  76.7 26.2 %all_to_all.15 = bf16[8,1,64,720]{3,2,1,0:T(8,128)(2,1)S(1)} all-to-all(bf16[8,1,64,720]{3,2,1,0:T(8,128)(2,1)S(1)} %bitcast.112), channel_id=1, replica_groups=mesh['rep'=2,'ep'=8,'tp'=2] {'ep'}, dimensions={0} | all-to-all | bytes 1474560 | tf_op jit(solution)/shard_map/all_to_all | solution.py:82
  102.9 0.2 pad_maximum_fusion
  103.0 5.0 %all_to_all.16 = bf16[2,8,1,64,720]{4,3,1,2,0:T(8,128)(2,1)S(1)} all-to-all(bf16[2,8,1,64,720]{4,3,1,2,0:T(8,128)(2,1)S(1)} %pad_maximum_fusion), channel_id=1, replica_groups=mesh['rep'=2,'ep'=8,'tp'=2] {'tp'}, dimensions={0} | all-to-all | bytes 2949120 | tf_op jit(solution)/shard_map/all_to_all | solution.py:80
  108.0 1.6 copy.60
  109.7 2.1 %reshape.100 = bf16[8,64,1440]{2,1,0:T(8,128)(2,1)} reshape(bf16[8,1,64,2,720]{4,3,2,0,1:T(2,128)(2,1)S(1)} %copy.60) | data formatting | bytes 2949120 | tf_op jit(solution)/shard_map/reshape.4
  111.8 4.8 %fusion.8 = f32[8,64,720]{2,1,0:T(8,128)} fusion(bf16[8,64,1440]{2,1,0:T(8,128)(2,1)} %reshape.100, bf16[1,1440,720]{2,1,0:T(8,128)(2,1)} %param.21), kind=kOutput, calls=%fused_computation.14 | convolution fusion | flops 1061683200 | bytes 5022720 | tf_op jit(solution)/shard_map/sekd,edf->sekf/dot_general | solution.py:91
  116.5 7.7 %convolution_bitcast_fusion = f32[8,1,64,1440]{3,2,0,1:T(8,128)} fusion(bf16[1,720,1440]{2,1,0:T(8,128)(2,1)} %param.23, bf16[8,64,1440]{2,1,0:T(8,128)(2,1)S(1)} %copy-done.2, bf16[1,1440,720]{2,1,0:T(8,128)(2,1)} %param.22, f32[8,64,720]{2,1,0:T(8,128)} %fusion.8), kind=kOutput, calls=%fused_computation.7 | convolution fusion | flops 2126315520 | bytes 10045440 | tf_op jit(solution)/shard_map/sekf,efd->sekd/dot_general | solution.py:98
  124.2 5.7 %copy.64 = f32[8,1,64,1440]{2,0,1,3:T(8,128)} copy(f32[8,1,64,1440]{3,2,0,1:T(8,128)} %convolution_bitcast_fusion) | data formatting | bytes 5898240
  129.9 5.9 %reshape.133 = f32[1440,512]{1,0:T(8,128)} reshape(f32[1440,1,8,64]{3,2,1,0:T(8,128)} %bitcast.108) | data formatting | bytes 5898240
  135.8 0.0 reduce-scatter.9.cloned.1.call-update
  135.8 10.1 %reduce-scatter.9.cloned.1.call-done = f32[720,512]{1,0:T(8,128)} async-done(((f32[1440,512]{1,0:T(8,128)}), f32[720,512]{1,0:T(8,128)}) %reduce-scatter.9.cloned.1.call-update) | async-done | bytes 1474576
  145.9 3.1 %reshape.134 = bf16[720,1,8,64]{3,2,1,0:T(8,128)(2,1)} reshape(f32[720,512]{1,0:T(8,128)} %reduce-scatter.9.cloned.1.call-done) | data formatting | bytes 2211840
  149.0 2.9 %copy.65 = bf16[8,1,64,720]{3,2,0,1:T(8,128)(2,1)} copy(bf16[8,1,64,720]{2,0,1,3:T(8,128)(2,1)} %bitcast.110) | data formatting | bytes 1474560
  151.9 26.3 %all_to_all.17 = bf16[8,1,64,720]{3,2,1,0:T(8,128)(2,1)S(1)} all-to-all(bf16[8,1,64,720]{3,2,1,0:T(8,128)(2,1)} %bitcast.113), channel_id=1, replica_groups=mesh['rep'=2,'ep'=8,'tp'=2] {'ep'}, dimensions={0} | all-to-all | bytes 1474560 | tf_op jit(solution)/shard_map/all_to_all | solution.py:102
  178.2 1.2 fusion.34
  (29 shorter events, 0.2 us)
Async XLA Ops:
  6.5 52.7 %copy-start = (bf16[1024,1440]{0,1:T(8,128)(2,1)S(1)}, bf16[1024,1440]{0,1:T(8,128)(2,1)}, u32[]{:S(2)}) copy-start(bf16[1024,1440]{0,1:T(8,128)(2,1)} %param.20) | copy-start | bytes 8847364
  6.5 6.7 %copy-start.7 = (s32[64,12]{0,1:T(8,128)S(1)}, s32[64,12]{0,1:T(8,128)}, u32[]{:S(2)}) copy-start(s32[64,12]{0,1:T(8,128)} %param.15) | copy-start | bytes 9220
  6.5 65.6 %reduce-scatter.7.cloned.1.call-start = ((), (), s32[]{:S(2)}) async-start(), calls=%async_computation.5 | async-start | bytes 1105920
  18.3 11.7 %copy-start.4 = (bf16[64,1024]{1,0:T(8,128)(2,1)S(1)}, bf16[64,1024]{1,0:T(8,128)(2,1)}, u32[]{:S(2)}) copy-start(bf16[64,1024]{1,0:T(8,128)(2,1)} %param.13) | copy-start | bytes 393220
  18.3 11.8 %copy-start.9 = (s32[64]{0:T(128)S(1)}, s32[64]{0:T(128)}, u32[]{:S(2)}) copy-start(s32[64]{0:T(128)} %param.16) | copy-start | bytes 772
  59.2 2.1 %copy-start.6 = (s32[64,4]{0,1:T(4,128)S(1)}, s32[64,4]{0,1:T(4,128)}, u32[]{:S(2)}) copy-start(s32[64,4]{0,1:T(4,128)} %param.17) | copy-start | bytes 3076
  59.2 3.5 %copy-start.8 = (f32[1440]{0:T(1024)S(1)}, f32[1440]{0:T(1024)}, u32[]{:S(2)}) copy-start(f32[1440]{0:T(1024)} %param.19) | copy-start | bytes 17284
  59.3 3.6 %copy-start.5 = (f32[64,4]{0,1:T(4,128)S(1)}, f32[64,4]{0,1:T(4,128)}, u32[]{:S(2)}) copy-start(f32[64,4]{0,1:T(4,128)} %param.18) | copy-start | bytes 3076
  59.3 14.0 %copy-start.3 = (bf16[64,1440]{1,0:T(8,128)(2,1)S(1)}, bf16[64,1440]{1,0:T(8,128)(2,1)}, u32[]{:S(2)}) copy-start(bf16[64,1440]{1,0:T(8,128)(2,1)} %param.12) | copy-start | bytes 552964
  61.1 84.8 %reduce-scatter.9.cloned.1.call-start = ((), (), s32[]{:S(2)}) async-start(), calls=%async_computation.6 | async-start | bytes 4423680
  111.8 4.8 %copy-start.2 = (bf16[8,64,1440]{2,1,0:T(8,128)(2,1)S(1)}, bf16[8,64,1440]{2,1,0:T(8,128)(2,1)}, u32[]{:S(2)}) copy-start(bf16[8,64,1440]{2,1,0:T(8,128)(2,1)} %reshape.100) | copy-start | bytes 4423684
  149.0 30.4 %copy-start.1 = (bf16[1024,1440]{0,1:T(8,128)(2,1)S(1)}, bf16[1024,1440]{0,1:T(8,128)(2,1)}, u32[]{:S(2)}) copy-start(bf16[1024,1440]{0,1:T(8,128)(2,1)} %param.20) | copy-start | bytes 8847364
Sparse Core Ops, SparseCore 0:
  61.2 10.8 reduce-scatter.6
  135.9 9.9 reduce-scatter.8
